TPU v7x, 256 devices: a whole 4x4x8 slice. The times are simulated.
256 devices in a mesh: chan: 64 (over y, z_hi, x), hour: 4 (over z_lo, core).
Axes of the slice: x: 4, y: 4, z: 8 (z_hi: 4, z_lo: 2; z = z_hi * 2 + z_lo), core: 2. Of those that a mesh axis runs over, the one named last changes fastest.
Arguments:
- spectra: bfloat16 [2, 64, 800, 8192], P(None, 'hour', None, 'chan'), may hold values from -6 to 6
- quality: int32 [64, 8192], P('hour', 'chan'), may hold values 0 or 1
- sources: int32 [32], replicated, may hold values from 0 to 8191
Outputs:
- correlation: bfloat16 [32, 512, 8192], P('hour', None, 'chan')
Inputs may be any that keep to these rules, and one draw needn't show every extreme that they name: `sources`: indices may repeat.
All inputs are finite; a program needn't handle non-finite values. No bound on the sum of `quality` on one device may be relied on, other than what follows from the above.
Results may differ from a plain program's by a relative error of at most 0.01.
Values may be sent and summed in bfloat16 or wider, within the bound.
A program may use at most 128 MiB of HBM per device.

v0:
```python
import math

import jax
import jax.numpy as jnp
from jax import lax
from jax.sharding import PartitionSpec as P

LAGS = 512


def whiten(record, usable):
    as_float = record.astype(jnp.float32)
    power = jnp.mean(as_float[0] * as_float[0] + as_float[1] * as_float[1], axis=1)
    scale = lax.rsqrt(power + 1e-06) * usable.astype(jnp.float32)
    return (as_float * scale[None, :, None, :]).astype(jnp.bfloat16)


def lag_table(freq_count, lag_count):
    bin_number = jnp.arange(freq_count, dtype=jnp.float32) + 1.0
    lag_offset = jnp.arange(lag_count, dtype=jnp.float32) - float(lag_count // 2)
    phase = math.pi * bin_number[:, None] * lag_offset[None, :] / freq_count
    return (jnp.stack([jnp.cos(phase), -jnp.sin(phase)]) / freq_count).astype(jnp.bfloat16)


def cross_spectrum(source_spec, receivers):
    real_part = jnp.einsum(
        "kwfs,kwfc->fsc", source_spec, receivers, preferred_element_type=jnp.float32
    )
    left_pair = jnp.stack([source_spec[0], -source_spec[1]])
    right_pair = jnp.stack([receivers[1], receivers[0]])
    imag_part = jnp.einsum(
        "kwfs,kwfc->fsc", left_pair, right_pair, preferred_element_type=jnp.float32
    )
    return jnp.stack([real_part, imag_part]).astype(jnp.bfloat16)


def body(spectra, quality, sources):
    channels_here = spectra.shape[3]
    freq_count = spectra.shape[2]
    whitened = whiten(spectra, quality)
    local_index = sources - lax.axis_index("chan") * channels_here
    onehot = (jnp.arange(channels_here, dtype=jnp.int32)[:, None] == local_index[None, :]).astype(
        jnp.bfloat16
    )
    picked = jnp.einsum("kwfc,cs->kwfs", whitened, onehot, preferred_element_type=jnp.float32)
    source_spec = lax.psum(picked, "chan").astype(jnp.bfloat16)
    partial_value = cross_spectrum(source_spec, whitened)
    table = lag_table(freq_count, LAGS)
    correlation = lax.psum_scatter(
        jnp.einsum("kfsc,kfl->slc", partial_value, table, preferred_element_type=jnp.float32),
        "hour",
        scatter_dimension=0,
        tiled=True,
    )
    return correlation.astype(jnp.bfloat16)


def solution(mesh):
    placed = (P(None, "hour", None, "chan"), P("hour", "chan"), P())
    return jax.shard_map(
        body, mesh=mesh, in_specs=placed, out_specs=P("hour", None, "chan"), check_vma=False
    )
```

profile of v0, /device:TPU:1, one launch (start us, length us, event | category | flops | bytes accessed | tf_op | source)
XLA Modules:
  0.0 635.2 jit_solution(4105570708778161971)
XLA Ops:
  6.5 0.0 reduce-scatter.2.cloned.1.call-start
  6.6 5.0 copy_convert_fusion
  11.5 0.0 copy-start.4
  11.5 0.9 fusion.3
  12.4 0.0 copy-done.4
  12.5 0.0 copy-start.5
  12.5 8.2 %multiply_convert_fusion = bf16[2,16,800,128]{3,1,0,2:T(8,128)(2,1)} fusion(f32[16,128]{1,0:T(8,128)S(1)} %convert_multiply_fusion, bf16[2,16,800,128]{3,2,1,0:T(8,128)(2,1)} %param.3), kind=kLoop, calls=%fused_computation.5 | loop fusion | flops 9830400 | bytes 13115392 | tf_op jit(solution)/shard_map/convert_element_type | solution.py:15
  20.6 0.0 copy-done.5
  20.6 11.3 %fusion.7 = f32[2,16,800,32]{2,3,1,0:T(8,128)} fusion(bf16[2,16,800,128]{3,1,0,2:T(8,128)(2,1)} %multiply_convert_fusion, s32[32]{0:T(128)S(1)} %broadcast_subtract_fusion), kind=kOutput, calls=%fused_computation.13 | convolution fusion | flops 209719296 | bytes 9830528 | tf_op jit(solution)/shard_map/kwfc,cs->kwfs/dot_general | solution.py:45
  31.9 378.3 %all-reduce.1 = bf16[2,16,800,32]{2,3,1,0:T(8,128)(2,1)S(1)} all-reduce(f32[2,16,800,32]{2,3,1,0:T(8,128)} %fusion.7), channel_id=1, replica_groups=mesh['chan'=64,'hour'=4] {'chan'}, use_global_device_ids=true, to_apply=%region_1.0 | all-reduce | flops 819200 | bytes 4915200 | tf_op jit(solution)/shard_map/psum | solution.py:46
  410.2 1.4 fusion.28
  411.6 10.3 %copy.6 = bf16[2,16,800,32]{3,1,0,2:T(8,128)(2,1)} copy(bf16[2,16,800,32]{2,3,1,0:T(8,128)(2,1)S(1)} %all-reduce.1) | data formatting | bytes 3276800 | tf_op jit(solution)/shard_map/convert_element_type | solution.py:46
  421.9 0.0 copy-start
  421.9 0.0 copy-start.1
  421.9 5.9 fusion.27
  427.7 0.0 copy-done
  427.7 0.0 copy-done.1
  427.7 1.5 pad_maximum_fusion.1
  429.2 10.9 %copy.7 = bf16[2,16,800,32]{3,1,0,2:T(8,128)(2,1)} copy(bf16[2,16,800,32]{2,3,1,0:T(8,128)(2,1)} %pad_maximum_fusion.1) | data formatting | bytes 3276800 | tf_op jit(solution)/shard_map/stack | solution.py:29
  440.1 9.8 %fusion.9 = bf16[1,800,32,128]{3,2,1,0:T(8,128)(2,1)} fusion(bf16[2,16,800,32]{3,1,0,2:T(8,128)(2,1)} %copy.6, bf16[2,16,800,128]{3,1,0,2:T(8,128)(2,1)} %multiply_convert_fusion), kind=kOutput, calls=%fused_computation.16 | convolution fusion | flops 212992000 | bytes 14745600 | tf_op jit(solution)/shard_map/kwfs,kwfc->fsc/dot_general | solution.py:26
  449.9 7.7 %fusion.20 = (f32[1,800,512]{2,1,0:T(8,128)}, f32[1,800,512]{2,1,0:T(8,128)}) fusion(f32[512]{0:T(512)S(1)} %iota_add_fusion, f32[800]{0:T(1024)S(1)} %add_multiply_fusion), kind=kLoop, calls=%fused_computation.26 | loop fusion | flops 1228800 | bytes 3282048 | tf_op jit(solution)/shard_map/cos | solution.py:22
  457.6 8.9 %fusion.10 = bf16[1,800,32,128]{3,2,1,0:T(8,128)(2,1)} fusion(bf16[2,16,800,32]{3,1,0,2:T(8,128)(2,1)} %copy.7, bf16[1,16,800,128]{3,1,0,2:T(8,128)(2,1)} %get-tuple-element.6, bf16[1,16,800,128]{3,1,0,2:T(8,128)(2,1)S(1)} %get-tuple-element.5), kind=kOutput, calls=%fused_computation.17 | convolution fusion | flops 216268800 | bytes 14745600 | tf_op jit(solution)/shard_map/kwfs,kwfc->fsc/dot_general | solution.py:31
  466.5 0.0 copy-start.2
  466.5 0.0 copy-start.3
  466.5 6.8 %pad_maximum_fusion = bf16[2,800,32,128]{3,2,1,0:T(8,128)(2,1)S(1)} fusion(bf16[1,800,32,128]{3,2,1,0:T(8,128)(2,1)} %fusion.10, bf16[1,800,32,128]{3,2,1,0:T(8,128)(2,1)} %fusion.9), kind=kLoop, calls=%fused_computation | loop fusion | flops 6553600 | bytes 26214400 | tf_op jit(solution)/shard_map/stack | solution.py:34
  473.2 0.0 copy-done.2
  473.2 0.0 copy-done.3
  473.3 21.3 %fusion.14 = f32[32,512,128]{2,1,0:T(8,128)} fusion(bf16[2,800,32,128]{3,2,1,0:T(8,128)(2,1)S(1)} %pad_maximum_fusion, f32[1,800,512]{2,1,0:T(8,128)S(1)} %copy-done.3, f32[1,800,512]{2,1,0:T(8,128)S(1)} %copy-done.2), kind=kOutput, calls=%fused_computation.20 | convolution fusion | flops 6713344000 | bytes 24772608 | tf_op jit(solution)/shard_map/kfsc,kfl->slc/dot_general | solution.py:50
  494.6 0.0 reduce-scatter.2.cloned.1.call-update
  494.6 131.0 %reduce-scatter.2.cloned.1.call-done = f32[8,512,128]{2,1,0:T(8,128)} async-done(((f32[32,512,128]{2,1,0:T(8,128)}), f32[8,512,128]{2,1,0:T(8,128)}) %reduce-scatter.2.cloned.1.call-update) | async-done | bytes 2097168 | tf_op jit(solution)/shard_map/reduce_scatter | solution.py:49
  625.6 2.7 convert_element_type.25
  (4 shorter events, 0.0 us)
Async XLA Ops:
  6.5 619.0 %reduce-scatter.2.cloned.1.call-start = ((), (), s32[]{:S(2)}) async-start(), calls=%async_computation.1 | async-start | bytes 10485760 | tf_op jit(solution)/shard_map/reduce_scatter | solution.py:49
  11.5 0.9 copy-start.4
  12.5 8.2 %copy-start.5 = (s32[32]{0:T(128)S(1)}, s32[32]{0:T(128)}, u32[]{:S(2)}) copy-start(s32[32]{0:T(128)} %param.5) | copy-start | bytes 388
  421.9 5.9 copy-start
  421.9 5.9 copy-start.1
  466.5 6.8 %copy-start.2 = (f32[1,800,512]{2,1,0:T(8,128)S(1)}, f32[1,800,512]{2,1,0:T(8,128)}, u32[]{:S(2)}) copy-start(f32[1,800,512]{2,1,0:T(8,128)} %get-tuple-element.9) | copy-start | bytes 4915204
  466.5 6.8 %copy-start.3 = (f32[1,800,512]{2,1,0:T(8,128)S(1)}, f32[1,800,512]{2,1,0:T(8,128)}, u32[]{:S(2)}) copy-start(f32[1,800,512]{2,1,0:T(8,128)} %get-tuple-element.10) | copy-start | bytes 4915204
Sparse Core Ops, SparseCore 0:
  494.7 130.7 reduce-scatter.1
where the time goes:
time: 635 us
  blocking collectives  378 us (60%)
  waiting for transfers between devices  131 us (21%)
  matrix products  51.3 us (8%)
  other arithmetic  34.1 us (5%)
  local copies, waits for them, and re-layouts  27.1 us (4%)
  between operations  13.5 us (2%)
    psum x1, blocking collectives, body(): source_spec = lax.psum(picked, 'chan').astype(jnp.bfloat16)  378 us
    reduce_scatter x1, waiting for transfers between devices, body(): lax.psum_scatter(jnp.einsum('kfsc,kfl->slc', partial_value, table, prefer...  131 us
    dot_general x1, matrix products, body(): jnp.einsum('kfsc,kfl->slc', partial_value, table, preferred_element_type=...  21.3 us
  transfers between devices with their start and end apart: 1, of which 1 were waited for; matrix products, arithmetic and copies ran while one was open for 0% of the time, Pallas kernels for 0%

commit v1 on v0

v1 whole, which is shorter than its diff:
```python
import jax
import jax.numpy as jnp
import numpy as np
from jax import lax
from jax.experimental import pallas as pl
from jax.experimental.pallas import tpu as pltpu
from jax.sharding import PartitionSpec as P

LAGS = 512
F32 = jnp.float32
BF16 = jnp.bfloat16
BLOCKS = 100
ROWS = 112
QUARTER = 28
PIECE = 7
DEPTH = 1664


def lag_table(freq_count):
    bin_number = np.arange(freq_count, dtype=np.float32) + np.float32(1.0)
    lag_offset = np.arange(LAGS, dtype=np.float32) - np.float32(LAGS // 2)
    phase = np.float32(np.pi) * bin_number[:, None] * lag_offset[None, :] / np.float32(freq_count)
    table = np.concatenate([np.cos(phase), -np.sin(phase)], 0) / np.float32(freq_count)
    table = np.concatenate([table, np.zeros((DEPTH - 2 * freq_count, LAGS), np.float32)], 0)
    return np.ascontiguousarray(table.T).astype(BF16)


def kernel(
    sources, spectra, quality, table_hbm, out_hbm,
    w, table, first, got1, sum1, got2, sum2, got3, sum3, got4, spec, part,
    to_core, from_core, to_chip, from_chip, kept, out,
    load_sem, table_sem, out_sem, send_sem, recv_sem, core_send, core_recv, chip_send, chip_recv,
):
    chan, hour = lax.axis_index("chan"), lax.axis_index("hour")
    y, zh, x = chan // 16, (chan // 4) % 4, chan % 4
    zl, core = hour // 2, hour % 2

    def at(ny, nzh, nx):
        return (ny * 16 + nzh * 4 + nx, hour)

    def along(axis, d):
        return at(y, zh, (x + d) % 4) if axis == 0 else at((y + d) % 4, zh, x)

    pair_a = at(y, zh + 1 - 2 * (zh % 2), x)
    pair_b = at(y, 3 - zh, x)
    core_peer = (chan, zl * 2 + 1 - core)
    chip_peer = (chan, (1 - zl) * 2 + core)

    loads = [
        pltpu.make_async_copy(
            spectra.at[kw // 16, kw % 16], w.at[:, pl.ds(kw * 8, 8), :], load_sem.at[kw]
        )
        for kw in range(32)
    ]
    for copy in loads:
        copy.start()
    load_table = pltpu.make_async_copy(table_hbm, table, table_sem)
    load_table.start()

    barrier = pltpu.get_barrier_semaphore()
    peers = [along(axis, d) for axis in range(2) for d in range(1, 4)]
    peers += [pair_a, pair_b, core_peer, chip_peer]
    for peer in peers:
        pl.semaphore_signal(barrier, inc=1, device_id=peer, device_id_type=pl.DeviceIdType.MESH)

    row = lax.broadcasted_iota(jnp.int32, (32, 128), 0)
    lane = lax.broadcasted_iota(jnp.int32, (32, 128), 1)
    wanted = jnp.zeros((32, 128), jnp.int32)
    for r in range(32):
        q, i = r // 8, r % 8
        chip = (1 - zl) if q < 2 else zl
        index = (chip * 2 + i // 4) * 8 + (q % 2) * 4 + i % 4
        wanted = jnp.where(row == r, sources[index], wanted)
    onehot = jnp.where(lane + chan * 128 == wanted, 1.0, 0.0).astype(BF16)
    usable = quality[...].astype(F32)
    usable_rows = jnp.broadcast_to(usable[:, None, :], (16, 8, 128)).reshape(128, 128)
    nt = (((1,), (1,)), ((), ()))
    usable_src = lax.dot_general(
        onehot, usable_rows.astype(BF16), nt, preferred_element_type=F32
    )
    zero_tile = jnp.zeros((8, 128), BF16)
    for q in range(4):
        for k in range(2):
            for fb in range(BLOCKS, ROWS):
                first[q, k, fb] = zero_tile
    part[:, pl.ds(1600, DEPTH - 1600), :] = jnp.zeros((4, DEPTH - 1600, 256), BF16)

    def pick(q0, q1):
        hot = onehot[q0 * 8:q1 * 8]
        use = usable_src[q0 * 8:q1 * 8]

        def step(fb, _):
            got = lax.dot_general(hot, w[fb], nt, preferred_element_type=F32)
            for q in range(q0, q1):
                rows = slice((q - q0) * 8, (q - q0 + 1) * 8)
                for k in range(2):
                    value = got[rows, k * 128:(k + 1) * 128] * use[rows]
                    first[q, k, fb] = value.astype(BF16)
            return 0

        lax.fori_loop(0, BLOCKS, step, 0, unroll=5)

    def send(src, dst, q, phase, k, d, peer):
        copy = pltpu.make_async_remote_copy(
            src_ref=src, dst_ref=dst,
            send_sem=send_sem.at[q, phase, k, d], recv_sem=recv_sem.at[q, phase, k, d],
            device_id=peer, device_id_type=pl.DeviceIdType.MESH,
        )
        copy.start()
        return copy

    sent = {}
    mine = [(x, y), (y, x)]

    def p1(q):
        for k in range(2):
            for d in range(1, 4):
                to = (mine[k][0] + d) % 4
                sent[q, 1, k, d] = send(
                    first.at[q, k, pl.ds(to * QUARTER, QUARTER)], got1.at[q, k, d - 1],
                    q, 0, k, d - 1, along(k, d),
                )

    def p2(q):
        for k in range(2):
            for d in range(1, 4):
                sent[q, 1, k, d].wait_recv()
            total = first[q, k, pl.ds(mine[k][0] * QUARTER, QUARTER)]
            for d in range(3):
                total = total + got1[q, k, d]
            sum1[q, k] = total
            for d in range(1, 4):
                to = (mine[k][1] + d) % 4
                sent[q, 2, k, d] = send(
                    sum1.at[q, k, pl.ds(to * PIECE, PIECE)], got2.at[q, k, d - 1],
                    q, 1, k, d - 1, along(1 - k, d),
                )

    def p3(q):
        for k in range(2):
            for d in range(1, 4):
                sent[q, 2, k, d].wait_recv()
            total = sum1[q, k, pl.ds(mine[k][1] * PIECE, PIECE)]
            for d in range(3):
                total = total + got2[q, k, d]
            sum2[q, k] = total
            sent[q, 3, k, 1] = send(
                sum2.at[q, k], got3.at[q, k], q, 2, k, 0, (pair_a, pair_b)[k]
            )

    def p4(q):
        for k in range(2):
            sent[q, 3, k, 1].wait_recv()
            sum3[q, k] = sum2[q, k] + got3[q, k]
            sent[q, 4, k, 1] = send(
                sum3.at[q, k], got4.at[q, k], q, 3, k, 0, (pair_b, pair_a)[k]
            )

    def p5(q):
        for k in range(2):
            sent[q, 4, k, 1].wait_recv()
            here = spec.at[q, k, pl.ds(mine[k][0] * QUARTER + mine[k][1] * PIECE, PIECE)]
            here[...] = sum3[q, k] + got4[q, k]
            for d in range(1, 4):
                sent[q, 5, k, d] = send(here, here, q, 4, k, d - 1, along(1 - k, d))

    def p6(q):
        for k in range(2):
            for d in range(1, 4):
                sent[q, 5, k, d].wait_recv()
            here = spec.at[q, k, pl.ds(mine[k][0] * QUARTER, QUARTER)]
            for d in range(1, 4):
                sent[q, 6, k, d] = send(here, here, q, 5, k, d - 1, along(k, d))

    def done(q):
        for k in range(2):
            for d in range(1, 4):
                sent[q, 6, k, d].wait_recv()

    def measure_power():
        def step(fb, total):
            value = w[fb].astype(F32)
            return total + value * value

        total = lax.fori_loop(0, BLOCKS, step, jnp.zeros((256, 128), F32), unroll=5)
        total = jnp.sum(total.reshape(32, 8, 128), axis=1)
        power = (total[:16] + total[16:]) / (BLOCKS * 8)
        scale = lax.rsqrt(power + 1e-06) * usable
        rows = jnp.broadcast_to(scale[:, None, :], (16, 8, 128)).reshape(128, 128)
        return jnp.concatenate([rows, rows], 0)

    def whiten(scale):
        def step(fb, _):
            w[fb] = (w[fb].astype(F32) * scale).astype(BF16)
            return 0

        lax.fori_loop(0, BLOCKS, step, 0, unroll=5)

    diagonal = (
        lax.broadcasted_iota(jnp.int32, (8, 128), 0)
        == lax.broadcasted_iota(jnp.int32, (8, 128), 1) % 8
    )
    same_window = jnp.where(
        lax.broadcasted_iota(jnp.int32, (128, 128), 0) // 8
        == lax.broadcasted_iota(jnp.int32, (128, 128), 1) // 8, 1.0, 0.0
    )

    def cross(q):
        def power_step(fb, total):
            real, imag = spec[q, 0, fb].astype(F32), spec[q, 1, fb].astype(F32)
            return total + real * real + imag * imag

        total = lax.fori_loop(0, BLOCKS, power_step, jnp.zeros((8, 128), F32), unroll=10)
        power = jnp.dot(
            total, same_window, precision=lax.Precision.HIGHEST, preferred_element_type=F32
        ) / (BLOCKS * 8)
        scale = lax.rsqrt(power + 1e-06)

        def step(pair, _):
            outs = []
            for d in range(2):
                fb = pair * 2 + d
                real = spec[q, 0, fb].astype(F32) * scale
                imag = spec[q, 1, fb].astype(F32) * scale
                upper, lower = [], []
                for s in range(8):
                    a = jnp.where(diagonal, jnp.broadcast_to(real[s:s + 1], (8, 128)), 0.0)
                    b = jnp.where(diagonal, jnp.broadcast_to(imag[s:s + 1], (8, 128)), 0.0)
                    upper.append(jnp.concatenate([a, b], 1))
                    lower.append(jnp.concatenate([-b, a], 1))
                left = jnp.concatenate(upper + lower, 0).astype(BF16)
                outs.append(jnp.dot(left, w[fb], preferred_element_type=F32).reshape(2, 8, 8, 128))
            for j in range(2):
                start = pl.multiple_of(j * 800 + pair * 16, 16)
                for s in range(8):
                    value = jnp.concatenate([outs[0][j, s], outs[1][j, s]], 0).astype(BF16)
                    part[s // 2, pl.ds(start, 16), pl.ds((s % 2) * 128, 128)] = value
            return 0

        lax.fori_loop(0, BLOCKS // 2, step, 0, unroll=5)

    def lags(pair):
        value = jnp.dot(table[...], part[pair], preferred_element_type=F32)
        return value[:, :128], value[:, 128:]

    moved = {}

    def stack(q):
        for i in range(2):
            both = lags((1 - core) * 2 + i)
            for s in range(2):
                to_core[q, i, s] = both[s].astype(BF16)
            copy = pltpu.make_async_remote_copy(
                src_ref=to_core.at[q, i], dst_ref=from_core.at[q, i],
                send_sem=core_send.at[q, i], recv_sem=core_recv.at[q, i],
                device_id=core_peer, device_id_type=pl.DeviceIdType.MESH,
            )
            copy.start()
            moved[q, i] = copy
        for i in range(2):
            both = lags(core * 2 + i)
            if q < 2:
                moved[q, i].wait_recv()
                for s in range(2):
                    to_chip[q, i, s] = (both[s] + from_core[q, i, s].astype(F32)).astype(BF16)
                copy = pltpu.make_async_remote_copy(
                    src_ref=to_chip.at[q, i], dst_ref=from_chip.at[q, i],
                    send_sem=chip_send.at[q, i], recv_sem=chip_recv.at[q, i],
                    device_id=chip_peer, device_id_type=pl.DeviceIdType.MESH,
                )
                copy.start()
                moved["chip", q, i] = copy
            else:
                for s in range(2):
                    kept[q - 2, i, s] = both[s]

    stores = []

    def finish(q, i):
        moved[q + 2, i].wait_recv()
        moved["chip", q, i].wait_recv()
        for s in range(2):
            value = kept[q, i, s] + from_core[q + 2, i, s].astype(F32)
            out[q, i, s] = (value + from_chip[q, i, s].astype(F32)).astype(BF16)
        copy = pltpu.make_async_copy(
            out.at[q, i], out_hbm.at[pl.ds(q * 4 + i * 2, 2)], out_sem.at[q, i]
        )
        copy.start()
        stores.append(copy)

    for copy in loads:
        copy.wait()
    pick(0, 1)
    pl.semaphore_wait(barrier, len(peers))
    p1(0)
    pick(1, 4)
    p2(0)
    p1(1)
    scale = measure_power()
    p3(0)
    whiten(scale)
    p4(0)
    p2(1)
    p1(2)
    p5(0)
    p3(1)
    p6(0)
    p4(1)
    p2(2)
    p1(3)
    done(0)
    p5(1)
    p3(2)
    p2(3)
    cross(0)
    p6(1)
    p4(2)
    p3(3)
    load_table.wait()
    stack(0)
    done(1)
    p5(2)
    p4(3)
    cross(1)
    p6(2)
    p5(3)
    stack(1)
    done(2)
    p6(3)
    cross(2)
    stack(2)
    done(3)
    cross(3)
    stack(3)
    for q in range(2):
        for i in range(2):
            finish(q, i)
    for copy in list(sent.values()) + list(moved.values()):
        copy.wait_send()
    for copy in stores:
        copy.wait()


def body(spectra, quality, sources):
    windows, freq_count, channels = spectra.shape[1:]
    any_space = pl.BlockSpec(memory_space=pl.ANY)
    dma = pltpu.SemaphoreType.DMA
    return pl.pallas_call(
        kernel,
        out_shape=jax.ShapeDtypeStruct((8, LAGS, channels), BF16),
        in_specs=[
            pl.BlockSpec(memory_space=pltpu.SMEM),
            any_space,
            pl.BlockSpec(memory_space=pltpu.VMEM),
            any_space,
        ],
        out_specs=any_space,
        scratch_shapes=[
            pltpu.VMEM((BLOCKS, 256, 128), BF16),
            pltpu.VMEM((LAGS, DEPTH), BF16),
            pltpu.VMEM((4, 2, ROWS, 8, 128), BF16),
            pltpu.VMEM((4, 2, 3, QUARTER, 8, 128), BF16),
            pltpu.VMEM((4, 2, QUARTER, 8, 128), BF16),
            pltpu.VMEM((4, 2, 3, PIECE, 8, 128), BF16),
            pltpu.VMEM((4, 2, PIECE, 8, 128), BF16),
            pltpu.VMEM((4, 2, PIECE, 8, 128), BF16),
            pltpu.VMEM((4, 2, PIECE, 8, 128), BF16),
            pltpu.VMEM((4, 2, PIECE, 8, 128), BF16),
            pltpu.VMEM((4, 2, ROWS, 8, 128), BF16),
            pltpu.VMEM((4, DEPTH, 256), BF16),
            pltpu.VMEM((4, 2, 2, LAGS, 128), BF16),
            pltpu.VMEM((4, 2, 2, LAGS, 128), BF16),
            pltpu.VMEM((2, 2, 2, LAGS, 128), BF16),
            pltpu.VMEM((2, 2, 2, LAGS, 128), BF16),
            pltpu.VMEM((2, 2, 2, LAGS, 128), F32),
            pltpu.VMEM((2, 2, 2, LAGS, 128), BF16),
            dma((32,)),
            dma,
            dma((2, 2)),
            dma((4, 6, 2, 3)),
            dma((4, 6, 2, 3)),
            dma((4, 2)),
            dma((4, 2)),
            dma((2, 2)),
            dma((2, 2)),
        ],
        compiler_params=pltpu.CompilerParams(
            collective_id=0, has_side_effects=True, vmem_limit_bytes=60 * 1024 * 1024
        ),
    )(
        sources,
        spectra.reshape(2, windows, BLOCKS, 8, channels),
        quality,
        jnp.asarray(lag_table(freq_count)),
    )


def solution(mesh):
    placed = (P(None, "hour", None, "chan"), P("hour", "chan"), P())
    return jax.shard_map(
        body, mesh=mesh, in_specs=placed, out_specs=P("hour", None, "chan"), check_vma=False
    )
```

time: 635 us -> 87.8 us (0.14)
  blocking collectives: 378 us -> 0 us
  waiting for transfers between devices: 131 us -> 0 us
  Pallas kernels: 0 us -> 85.4 us
  matrix products: 51.3 us -> 0 us
  other arithmetic: 34.1 us -> 0 us
  local copies, waits for them, and re-layouts: 27.1 us -> 2.27 us
  between operations: 13.5 us -> 0.01 us
    psum x1 -> x0, blocking collectives: 378 us -> none  [body(): source_spec = lax.psum(picked, 'chan').astype(jnp.bfloat16)]
    reduce_scatter x1 -> x0, waiting for transfers between devices: 131 us -> none  [body(): lax.psum_scatter(jnp.einsum('kfsc,kfl->slc', partial_value, table, prefer...]
    pallas_call x0 -> x1, Pallas kernels: none -> 85.4 us  [body(): pl.pallas_call(kernel, out_shape=jax.ShapeDtypeStruct((8, LAGS, channels)...]
    dot_general x4 -> x0, matrix products: 51.3 us -> none  [the longest x1 21.3 us: body(): jnp.einsum('kfsc,kfl->slc', partial_value, table, preferred_element_type=...]
    convert_element_type x3 -> x0, other arithmetic: 15.9 us -> none  [the longest x1 8.15 us: whiten(): return (as_float * scale[None, :, None, :]).astype(jnp.bfloat16)]
    another operation x1 -> x0, local copies, waits for them, and re-layouts: 10.9 us -> none  [cross_spectrum(): left_pair = jnp.stack([source_spec[0], -source_spec[1]])]
    convert_element_type x1 -> x0, local copies, waits for them, and re-layouts: 10.3 us -> none  [body(): source_spec = lax.psum(picked, 'chan').astype(jnp.bfloat16)]
    another operation x2 -> x0, other arithmetic: 8.24 us -> none  [the longest x1 6.75 us: cross_spectrum(): return jnp.stack([real_part, imag_part]).astype(jnp.bfloat16)]
  transfers between devices with their start and end apart: 1 -> 0, of which waited for: 1 -> 0; matrix products, arithmetic and copies ran while one was open for 0% -> 0% of each run, Pallas kernels for 0% -> 0%
where the time goes in v1:
time: 87.8 us; the launch traced here: 87.6 us
  Pallas kernels  85.4 us (97%)
  local copies, waits for them, and re-layouts  2.27 us (3%)
    pallas_call x1, Pallas kernels, body(): pl.pallas_call(kernel, out_shape=jax.ShapeDtypeStruct((8, LAGS, channels)...  85.4 us
    unnamed x1, local copies, waits for them, and re-layouts  2.27 us

profile of v1, /device:TPU:1, one launch (start us, length us, event | category | flops | bytes accessed | tf_op | source)
XLA Modules:
  0.0 87.6 jit_solution(13882229092858240521)
XLA Ops:
  0.0 85.4 %shard_map.46 = bf16[8,512,128]{2,1,0:T(8,128)(2,1)} custom-call(s32[32]{0:T(128)} %sources.1, bf16[2,16,100,8,128]{4,3,2,1,0:T(8,128)(2,1)} %bitcast.1, s32[16,128]{1,0:T(8,128)} %quality.1, bf16[512,1664]{1,0:T(8,128)(2,1)} %constant.2.clone.table_hbm), custom_call_target="tpu_custom_call" | custom-call | tf_op jit(solution)/shard_map/pallas_call | solution.py:348
  85.4 2.3 %copy.6 = bf16[8,512,128]{2,1,0:T(8,128)(2,1)} copy(bf16[8,512,128]{2,1,0:T(8,128)(2,1)} %shard_map.46) | data formatting | bytes 2097152

commit v2 on v1

--- a/solution.py
+++ b/solution.py
@@ -27,7 +27,7 @@
 
 def kernel(
     sources, spectra, quality, table_hbm, out_hbm,
-    w, table, first, got1, sum1, got2, sum2, got3, sum3, got4, spec, part,
+    w, table, first, got1, sum1, got2, sum2, got3, spec, part,
     to_core, from_core, to_chip, from_chip, kept, out,
     load_sem, table_sem, out_sem, send_sem, recv_sem, core_send, core_recv, chip_send, chip_recv,
 ):
@@ -38,28 +38,33 @@
     def at(ny, nzh, nx):
         return (ny * 16 + nzh * 4 + nx, hour)
 
+    quarters = [(r * QUARTER, min(QUARTER, BLOCKS - r * QUARTER)) for r in range(4)]
+
     def along(axis, d):
         return at(y, zh, (x + d) % 4) if axis == 0 else at((y + d) % 4, zh, x)
 
-    pair_a = at(y, zh + 1 - 2 * (zh % 2), x)
-    pair_b = at(y, 3 - zh, x)
     core_peer = (chan, zl * 2 + 1 - core)
     chip_peer = (chan, (1 - zl) * 2 + core)
 
     loads = [
-        pltpu.make_async_copy(
-            spectra.at[kw // 16, kw % 16], w.at[:, pl.ds(kw * 8, 8), :], load_sem.at[kw]
-        )
-        for kw in range(32)
+        [
+            pltpu.make_async_copy(
+                spectra.at[kw // 16, kw % 16, pl.ds(low, size)],
+                w.at[pl.ds(low, size), pl.ds(kw * 8, 8), :], load_sem.at[r, kw],
+            )
+            for kw in range(32)
+        ]
+        for r, (low, size) in enumerate(quarters)
     ]
-    for copy in loads:
-        copy.start()
+    for group in loads:
+        for copy in group:
+            copy.start()
     load_table = pltpu.make_async_copy(table_hbm, table, table_sem)
     load_table.start()
 
     barrier = pltpu.get_barrier_semaphore()
     peers = [along(axis, d) for axis in range(2) for d in range(1, 4)]
-    peers += [pair_a, pair_b, core_peer, chip_peer]
+    peers += [at(y, (zh + d) % 4, x) for d in range(1, 4)] + [core_peer, chip_peer]
     for peer in peers:
         pl.semaphore_signal(barrier, inc=1, device_id=peer, device_id_type=pl.DeviceIdType.MESH)
 
@@ -85,7 +90,7 @@
                 first[q, k, fb] = zero_tile
     part[:, pl.ds(1600, DEPTH - 1600), :] = jnp.zeros((4, DEPTH - 1600, 256), BF16)
 
-    def pick(q0, q1):
+    def pick(q0, q1, low, high):
         hot = onehot[q0 * 8:q1 * 8]
         use = usable_src[q0 * 8:q1 * 8]
 
@@ -98,7 +103,7 @@
                     first[q, k, fb] = value.astype(BF16)
             return 0
 
-        lax.fori_loop(0, BLOCKS, step, 0, unroll=5)
+        lax.fori_loop(low, high, step, 0, unroll=4)
 
     def send(src, dst, q, phase, k, d, peer):
         copy = pltpu.make_async_remote_copy(
@@ -112,14 +117,30 @@
     sent = {}
     mine = [(x, y), (y, x)]
 
+    def p1_copy(q, k, to, slot):
+        peer = at(y, zh, to) if k == 0 else at(to, zh, x)
+        return pltpu.make_async_remote_copy(
+            src_ref=first.at[q, k, pl.ds(to * QUARTER, QUARTER)], dst_ref=got1.at[q, k, slot],
+            send_sem=send_sem.at[q, 0, k, slot], recv_sem=recv_sem.at[q, 0, k, slot],
+            device_id=peer, device_id_type=pl.DeviceIdType.MESH,
+        )
+
+    def p1_quarter(q, r):
+        for k in range(2):
+            @pl.when(mine[k][0] != r)
+            def _():
+                p1_copy(q, k, r, (r + 3 - mine[k][0]) % 4).start()
+
+    def p1_expect(q):
+        for k in range(2):
+            for d in range(1, 4):
+                sent[q, 1, k, d] = p1_copy(q, k, (mine[k][0] + d) % 4, d - 1)
+
     def p1(q):
-        for k in range(2):
-            for d in range(1, 4):
-                to = (mine[k][0] + d) % 4
-                sent[q, 1, k, d] = send(
-                    first.at[q, k, pl.ds(to * QUARTER, QUARTER)], got1.at[q, k, d - 1],
-                    q, 0, k, d - 1, along(k, d),
-                )
+        p1_expect(q)
+        for k in range(2):
+            for d in range(1, 4):
+                sent[q, 1, k, d].start()
 
     def p2(q):
         for k in range(2):
@@ -144,23 +165,20 @@
             for d in range(3):
                 total = total + got2[q, k, d]
             sum2[q, k] = total
-            sent[q, 3, k, 1] = send(
-                sum2.at[q, k], got3.at[q, k], q, 2, k, 0, (pair_a, pair_b)[k]
-            )
-
-    def p4(q):
-        for k in range(2):
-            sent[q, 3, k, 1].wait_recv()
-            sum3[q, k] = sum2[q, k] + got3[q, k]
-            sent[q, 4, k, 1] = send(
-                sum3.at[q, k], got4.at[q, k], q, 3, k, 0, (pair_b, pair_a)[k]
-            )
+            for d in (2, 1, 3):
+                sent[q, 3, k, d] = send(
+                    sum2.at[q, k], got3.at[q, k, d - 1], q, 2, k, d - 1, at(y, (zh + d) % 4, x)
+                )
 
     def p5(q):
         for k in range(2):
-            sent[q, 4, k, 1].wait_recv()
+            for d in range(1, 4):
+                sent[q, 3, k, d].wait_recv()
+            total = sum2[q, k]
+            for d in range(3):
+                total = total + got3[q, k, d]
             here = spec.at[q, k, pl.ds(mine[k][0] * QUARTER + mine[k][1] * PIECE, PIECE)]
-            here[...] = sum3[q, k] + got4[q, k]
+            here[...] = total
             for d in range(1, 4):
                 sent[q, 5, k, d] = send(here, here, q, 4, k, d - 1, along(1 - k, d))
 
@@ -288,45 +306,44 @@
         copy.start()
         stores.append(copy)
 
-    for copy in loads:
-        copy.wait()
-    pick(0, 1)
-    pl.semaphore_wait(barrier, len(peers))
-    p1(0)
-    pick(1, 4)
+    for r, (low, size) in enumerate(quarters):
+        for copy in loads[r]:
+            copy.wait()
+        pick(0, 1, low, low + size)
+        if r == 0:
+            pl.semaphore_wait(barrier, len(peers))
+        p1_quarter(0, r)
+    p1_expect(0)
+    pick(1, 4, 0, BLOCKS)
+    p1(1)
     p2(0)
-    p1(1)
     scale = measure_power()
     p3(0)
-    whiten(scale)
-    p4(0)
     p2(1)
     p1(2)
+    p1(3)
+    whiten(scale)
     p5(0)
     p3(1)
+    p2(2)
     p6(0)
-    p4(1)
-    p2(2)
-    p1(3)
+    p5(1)
+    p2(3)
+    p3(2)
     done(0)
-    p5(1)
-    p3(2)
-    p2(3)
+    p6(1)
+    p3(3)
+    p5(2)
     cross(0)
-    p6(1)
-    p4(2)
-    p3(3)
+    p5(3)
+    p6(2)
     load_table.wait()
     stack(0)
     done(1)
-    p5(2)
-    p4(3)
     cross(1)
-    p6(2)
-    p5(3)
+    p6(3)
     stack(1)
     done(2)
-    p6(3)
     cross(2)
     stack(2)
     done(3)
@@ -363,9 +380,7 @@
             pltpu.VMEM((4, 2, QUARTER, 8, 128), BF16),
             pltpu.VMEM((4, 2, 3, PIECE, 8, 128), BF16),
             pltpu.VMEM((4, 2, PIECE, 8, 128), BF16),
-            pltpu.VMEM((4, 2, PIECE, 8, 128), BF16),
-            pltpu.VMEM((4, 2, PIECE, 8, 128), BF16),
-            pltpu.VMEM((4, 2, PIECE, 8, 128), BF16),
+            pltpu.VMEM((4, 2, 3, PIECE, 8, 128), BF16),
             pltpu.VMEM((4, 2, ROWS, 8, 128), BF16),
             pltpu.VMEM((4, DEPTH, 256), BF16),
             pltpu.VMEM((4, 2, 2, LAGS, 128), BF16),
@@ -374,7 +389,7 @@
             pltpu.VMEM((2, 2, 2, LAGS, 128), BF16),
             pltpu.VMEM((2, 2, 2, LAGS, 128), F32),
             pltpu.VMEM((2, 2, 2, LAGS, 128), BF16),
-            dma((32,)),
+            dma((4, 32)),
             dma,
             dma((2, 2)),
             dma((4, 6, 2, 3)),

time: 87.8 us -> 80 us (0.911)
  Pallas kernels: 85.4 us -> 77.5 us
    pallas_call x1, Pallas kernels: 85.4 us -> 77.5 us  [body(): pl.pallas_call(kernel, out_shape=jax.ShapeDtypeStruct((8, LAGS, channels)...]
where the time goes in v2:
time: 80 us; the launch traced here: 79.8 us
  Pallas kernels  77.5 us (97%)
  local copies, waits for them, and re-layouts  2.27 us (3%)
    pallas_call x1, Pallas kernels, body(): pl.pallas_call(kernel, out_shape=jax.ShapeDtypeStruct((8, LAGS, channels)...  77.5 us
    unnamed x1, local copies, waits for them, and re-layouts  2.27 us

profile of v2, /device:TPU:1, one launch (start us, length us, event | category | flops | bytes accessed | tf_op | source)
XLA Modules:
  0.0 79.8 jit_solution(7985094713112026814)
XLA Ops:
  0.0 77.5 %shard_map.46 = bf16[8,512,128]{2,1,0:T(8,128)(2,1)} custom-call(s32[32]{0:T(128)} %sources.1, bf16[2,16,100,8,128]{4,3,2,1,0:T(8,128)(2,1)} %bitcast.1, s32[16,128]{1,0:T(8,128)} %quality.1, bf16[512,1664]{1,0:T(8,128)(2,1)} %constant.2.clone.table_hbm), custom_call_target="tpu_custom_call" | custom-call | tf_op jit(solution)/shard_map/pallas_call | solution.py:365
  77.5 2.3 %copy.6 = bf16[8,512,128]{2,1,0:T(8,128)(2,1)} copy(bf16[8,512,128]{2,1,0:T(8,128)(2,1)} %shard_map.46) | data formatting | bytes 2097152

commit v3 on v2

--- a/solution.py
+++ b/solution.py
@@ -45,6 +45,12 @@
 
     core_peer = (chan, zl * 2 + 1 - core)
     chip_peer = (chan, (1 - zl) * 2 + core)
+
+    barrier = pltpu.get_barrier_semaphore()
+    peers = [along(axis, d) for axis in range(2) for d in range(1, 4)]
+    peers += [at(y, (zh + d) % 4, x) for d in range(1, 4)] + [core_peer, chip_peer]
+    for peer in peers:
+        pl.semaphore_signal(barrier, inc=1, device_id=peer, device_id_type=pl.DeviceIdType.MESH)
 
     loads = [
         [
@@ -61,12 +67,6 @@
             copy.start()
     load_table = pltpu.make_async_copy(table_hbm, table, table_sem)
     load_table.start()
-
-    barrier = pltpu.get_barrier_semaphore()
-    peers = [along(axis, d) for axis in range(2) for d in range(1, 4)]
-    peers += [at(y, (zh + d) % 4, x) for d in range(1, 4)] + [core_peer, chip_peer]
-    for peer in peers:
-        pl.semaphore_signal(barrier, inc=1, device_id=peer, device_id_type=pl.DeviceIdType.MESH)
 
     row = lax.broadcasted_iota(jnp.int32, (32, 128), 0)
     lane = lax.broadcasted_iota(jnp.int32, (32, 128), 1)
@@ -309,39 +309,38 @@
     for r, (low, size) in enumerate(quarters):
         for copy in loads[r]:
             copy.wait()
-        pick(0, 1, low, low + size)
+        pick(0, 4, low, low + size)
         if r == 0:
             pl.semaphore_wait(barrier, len(peers))
         p1_quarter(0, r)
     p1_expect(0)
-    pick(1, 4, 0, BLOCKS)
     p1(1)
     p2(0)
-    scale = measure_power()
-    p3(0)
     p2(1)
     p1(2)
     p1(3)
+    scale = measure_power()
+    p3(0)
+    p3(1)
     whiten(scale)
     p5(0)
-    p3(1)
     p2(2)
-    p6(0)
     p5(1)
     p2(3)
+    p6(0)
     p3(2)
-    done(0)
     p6(1)
     p3(3)
+    done(0)
+    cross(0)
     p5(2)
-    cross(0)
     p5(3)
-    p6(2)
     load_table.wait()
     stack(0)
+    p6(2)
+    p6(3)
     done(1)
     cross(1)
-    p6(3)
     stack(1)
     done(2)
     cross(2)
@@ -400,7 +399,7 @@
             dma((2, 2)),
         ],
         compiler_params=pltpu.CompilerParams(
-            collective_id=0, has_side_effects=True, vmem_limit_bytes=60 * 1024 * 1024
+            collective_id=0, has_side_effects=True, vmem_limit_bytes=52 * 1024 * 1024
         ),
     )(
         sources,

time: 80 us -> 75.5 us (0.944)
  Pallas kernels: 77.5 us -> 73.1 us
    pallas_call x1, Pallas kernels: 77.5 us -> 73.1 us  [body(): pl.pallas_call(kernel, out_shape=jax.ShapeDtypeStruct((8, LAGS, channels)...]
    unnamed x1 -> x5, local copies, waits for them, and re-layouts: 2.27 us -> 2.32 us
where the time goes in v3:
time: 75.5 us; the launch traced here: 75.4 us
  Pallas kernels  73.1 us (97%)
  local copies, waits for them, and re-layouts  2.32 us (3%)
    pallas_call x1, Pallas kernels, body(): pl.pallas_call(kernel, out_shape=jax.ShapeDtypeStruct((8, LAGS, channels)...  73.1 us
    unnamed x5, local copies, waits for them, and re-layouts  2.32 us

profile of v3, /device:TPU:1, one launch (start us, length us, event | category | flops | bytes accessed | tf_op | source)
XLA Modules:
  0.0 75.4 jit_solution(7736907816620913178)
XLA Ops:
  0.0 0.0 copy-start
  0.0 0.7 copy-done
  0.7 0.0 copy-start.1
  0.7 0.7 copy-done.1
  1.4 73.1 %shard_map.46 = bf16[8,512,128]{2,1,0:T(8,128)(2,1)S(1)} custom-call(s32[32]{0:T(128)S(1)} %copy-done.1, bf16[2,16,100,8,128]{4,3,2,1,0:T(8,128)(2,1)} %bitcast.1, s32[16,128]{1,0:T(8,128)S(1)} %copy-done, bf16[512,1664]{1,0:T(8,128)(2,1)} %constant.2.clone.table_hbm), custom_call_target="tpu_custom_call" | custom-call | tf_op jit(solution)/shard_map/pallas_call | solution.py:364
  74.4 1.0 %copy.6 = bf16[8,512,128]{2,1,0:T(8,128)(2,1)} copy(bf16[8,512,128]{2,1,0:T(8,128)(2,1)S(1)} %shard_map.46) | data formatting | bytes 2097152
Async XLA Ops:
  0.0 0.7 copy-start
  0.7 0.7 copy-start.1

commit v4 on v3

--- a/solution.py
+++ b/solution.py
@@ -255,7 +255,7 @@
                     part[s // 2, pl.ds(start, 16), pl.ds((s % 2) * 128, 128)] = value
             return 0
 
-        lax.fori_loop(0, BLOCKS // 2, step, 0, unroll=5)
+        lax.fori_loop(0, BLOCKS // 2, step, 0, unroll=10)
 
     def lags(pair):
         value = jnp.dot(table[...], part[pair], preferred_element_type=F32)

time: 75.5 us -> 73.3 us (0.971)
  Pallas kernels: 73.1 us -> 70.8 us
    pallas_call x1, Pallas kernels: 73.1 us -> 70.8 us  [body(): pl.pallas_call(kernel, out_shape=jax.ShapeDtypeStruct((8, LAGS, channels)...]
where the time goes in v4:
time: 73.3 us; the launch traced here: 73.2 us
  Pallas kernels  70.8 us (97%)
  local copies, waits for them, and re-layouts  2.32 us (3%)
    pallas_call x1, Pallas kernels, body(): pl.pallas_call(kernel, out_shape=jax.ShapeDtypeStruct((8, LAGS, channels)...  70.8 us
    unnamed x5, local copies, waits for them, and re-layouts  2.32 us

profile of v4, /device:TPU:1, one launch (start us, length us, event | category | flops | bytes accessed | tf_op | source)
XLA Modules:
  0.0 73.2 jit_solution(5048857335488106988)
XLA Ops:
  0.0 0.0 copy-start
  0.0 0.7 copy-done
  0.7 0.0 copy-start.1
  0.7 0.7 copy-done.1
  1.4 70.8 %shard_map.46 = bf16[8,512,128]{2,1,0:T(8,128)(2,1)S(1)} custom-call(s32[32]{0:T(128)S(1)} %copy-done.1, bf16[2,16,100,8,128]{4,3,2,1,0:T(8,128)(2,1)} %bitcast.1, s32[16,128]{1,0:T(8,128)S(1)} %copy-done, bf16[512,1664]{1,0:T(8,128)(2,1)} %constant.2.clone.table_hbm), custom_call_target="tpu_custom_call" | custom-call | tf_op jit(solution)/shard_map/pallas_call | solution.py:364
  72.2 1.0 %copy.6 = bf16[8,512,128]{2,1,0:T(8,128)(2,1)} copy(bf16[8,512,128]{2,1,0:T(8,128)(2,1)S(1)} %shard_map.46) | data formatting | bytes 2097152
Async XLA Ops:
  0.0 0.7 copy-start
  0.7 0.7 copy-start.1

commit v5 on v4

--- a/solution.py
+++ b/solution.py
@@ -255,7 +255,7 @@
                     part[s // 2, pl.ds(start, 16), pl.ds((s % 2) * 128, 128)] = value
             return 0
 
-        lax.fori_loop(0, BLOCKS // 2, step, 0, unroll=10)
+        lax.fori_loop(0, BLOCKS // 2, step, 0, unroll=25)
 
     def lags(pair):
         value = jnp.dot(table[...], part[pair], preferred_element_type=F32)

time: 73.3 us -> 72.9 us (level)
  no operation moved by 1% of the time
where the time goes in v5:
time: 72.9 us; the launch traced here: 72.7 us
  Pallas kernels  70.4 us (97%)
  local copies, waits for them, and re-layouts  2.32 us (3%)
    pallas_call x1, Pallas kernels, body(): pl.pallas_call(kernel, out_shape=jax.ShapeDtypeStruct((8, LAGS, channels)...  70.4 us
    unnamed x5, local copies, waits for them, and re-layouts  2.32 us

profile of v5, /device:TPU:1, one launch (start us, length us, event | category | flops | bytes accessed | tf_op | source)
XLA Modules:
  0.0 72.7 jit_solution(10581547317289098414)
XLA Ops:
  0.0 0.0 copy-start
  0.0 0.7 copy-done
  0.7 0.0 copy-start.1
  0.7 0.7 copy-done.1
  1.4 70.4 %shard_map.46 = bf16[8,512,128]{2,1,0:T(8,128)(2,1)S(1)} custom-call(s32[32]{0:T(128)S(1)} %copy-done.1, bf16[2,16,100,8,128]{4,3,2,1,0:T(8,128)(2,1)} %bitcast.1, s32[16,128]{1,0:T(8,128)S(1)} %copy-done, bf16[512,1664]{1,0:T(8,128)(2,1)} %constant.2.clone.table_hbm), custom_call_target="tpu_custom_call" | custom-call | tf_op jit(solution)/shard_map/pallas_call | solution.py:364
  71.7 1.0 %copy.6 = bf16[8,512,128]{2,1,0:T(8,128)(2,1)} copy(bf16[8,512,128]{2,1,0:T(8,128)(2,1)S(1)} %shard_map.46) | data formatting | bytes 2097152
Async XLA Ops:
  0.0 0.7 copy-start
  0.7 0.7 copy-start.1
